TPU v7x, 128 devices: a whole 4x4x4 slice. The times are simulated.
128 devices in a mesh: blk: 32 (over z_lo, y, x), head: 4 (over z_hi, core).
Axes of the slice: x: 4, y: 4, z: 4 (z_hi: 2, z_lo: 2; z = z_hi * 2 + z_lo), core: 2. Of those that a mesh axis runs over, the one named last changes fastest.
Arguments:
- query_vectors: bfloat16 [4096, 2560], P('blk', 'head'), may hold values from -8 to 8
- key_vectors: bfloat16 [4096, 2560], P('blk', 'head'), may hold values from -8 to 8, as said below
- value_vectors: bfloat16 [4096, 2560], P('blk', 'head'), may hold values from -6 to 6
- tangent_queries: bfloat16 [4096, 2560], P('blk', 'head'), may hold values from -6 to 6
- tangent_keys: bfloat16 [4096, 2560], P('blk', 'head'), may hold values from -6 to 6
- tangent_values: bfloat16 [4096, 2560], P('blk', 'head'), may hold values from -6 to 6
- target_gap: bfloat16 [4096, 2560], P(('blk', 'head')), may hold values from -6 to 6
Outputs:
- primal_out: bfloat16 [4096, 2560], P(('blk', 'head'))
- tangent_out: bfloat16 [4096, 2560], P(('blk', 'head'))
- query_grad: bfloat16 [4096, 2560], P('blk', 'head')
- key_grad: bfloat16 [4096, 2560], P('blk', 'head')
- value_grad: bfloat16 [4096, 2560], P('blk', 'head')
Inputs may be any that keep to these rules, and one draw needn't show every extreme that they name: `key_vectors`: keys are real-valued draws.
All inputs are finite; a program needn't handle non-finite values.
Results may differ from a plain program's by a relative error of at most 0.015.
Values may be sent and summed in bfloat16 or wider, within the bound.
No kernel may reach another device: no remote copies, remote signals or barrier semaphores. Data moves between devices by JAX's collectives and lax.ppermute only.
A program may use at most 128 MiB of HBM per device.

v0:
```python
from functools import partial
import math
import jax
import jax.numpy as jnp
from jax import lax
from jax.sharding import PartitionSpec as P

HD = 128
scale_loss = 64.0
floor_value = -1e30


def split_heads(matrix, head_count):
    return matrix.reshape(matrix.shape[0], head_count, matrix.shape[1] // head_count)


def fold_blocks(advance, running, operands, length):
    block_rows = length
    while block_rows > 512 and block_rows % 2 == 0:
        block_rows = block_rows // 2
    block_total = length // block_rows

    def one_block(position, carried):
        slices = tuple(
            (
                lax.dynamic_slice_in_dim(member, position * block_rows, block_rows, 0)
                for member in operands
            )
        )
        return advance(carried, slices)

    return lax.fori_loop(0, block_total, one_block, running)


def forward_update(nearby, running, slices):
    near_queries, near_tangents, inverse = nearby
    far_keys, far_values, far_tan_keys, far_tan_values = slices
    row_peak, denominator, tan_weight, primal_sum, tangent_sum = running
    scores = (
        jnp.einsum("qhd,khd->qhk", near_queries, far_keys, preferred_element_type=jnp.float32)
        * inverse
    )
    tan_scores = (
        jnp.einsum("qhd,khd->qhk", near_tangents, far_keys, preferred_element_type=jnp.float32)
        + jnp.einsum("qhd,khd->qhk", near_queries, far_tan_keys, preferred_element_type=jnp.float32)
    ) * inverse
    new_peak = jnp.maximum(row_peak, jnp.max(scores, axis=2))
    factor = jnp.exp(row_peak - new_peak)
    weights = jnp.exp(scores - new_peak[:, :, None])
    weighted_tan = weights * tan_scores
    denominator = factor * denominator + jnp.sum(weights, axis=2)
    tan_weight = factor * tan_weight + jnp.sum(weighted_tan, axis=2)
    weights_low = weights.astype(jnp.bfloat16)
    tan_low = weighted_tan.astype(jnp.bfloat16)
    primal_sum = factor[:, :, None] * primal_sum + jnp.einsum(
        "qhk,khd->qhd", weights_low, far_values, preferred_element_type=jnp.float32
    )
    tangent_sum = (
        factor[:, :, None] * tangent_sum
        + jnp.einsum("qhk,khd->qhd", tan_low, far_values, preferred_element_type=jnp.float32)
        + jnp.einsum(
            "qhk,khd->qhd", weights_low, far_tan_values, preferred_element_type=jnp.float32
        )
    )
    return (new_peak, denominator, tan_weight, primal_sum, tangent_sum)


def query_update(nearby, running, slices):
    near_queries, near_cotangent, log_total, inner_sums, inverse = nearby
    far_keys, far_values = slices
    scores = (
        jnp.einsum("qhd,khd->qhk", near_queries, far_keys, preferred_element_type=jnp.float32)
        * inverse
    )
    chances = jnp.exp(scores - log_total[:, :, None])
    prob_grad = jnp.einsum(
        "qhd,khd->qhk", near_cotangent, far_values, preferred_element_type=jnp.float32
    )
    score_grad = (chances * (prob_grad - inner_sums[:, :, None])).astype(jnp.bfloat16)
    return running + jnp.einsum(
        "qhk,khd->qhd", score_grad, far_keys, preferred_element_type=jnp.float32
    )


def key_update(nearby, running, slices):
    near_keys, near_values, inverse = nearby
    far_queries, far_cotangent, far_log, far_inner = slices
    key_acc, value_acc = running
    scores = (
        jnp.einsum("qhd,khd->qhk", far_queries, near_keys, preferred_element_type=jnp.float32)
        * inverse
    )
    chances = jnp.exp(scores - far_log[:, :, None])
    value_acc = value_acc + jnp.einsum(
        "qhk,qhd->khd",
        chances.astype(jnp.bfloat16),
        far_cotangent,
        preferred_element_type=jnp.float32,
    )
    prob_grad = jnp.einsum(
        "qhd,khd->qhk", far_cotangent, near_values, preferred_element_type=jnp.float32
    )
    score_grad = (chances * (prob_grad - far_inner[:, :, None])).astype(jnp.bfloat16)
    key_acc = key_acc + jnp.einsum(
        "qhk,qhd->khd", score_grad, far_queries, preferred_element_type=jnp.float32
    )
    return (key_acc, value_acc)


def per_device(
    query_vectors,
    key_vectors,
    value_vectors,
    tangent_queries,
    tangent_keys,
    tangent_values,
    target_gap,
):
    local_rows = query_vectors.shape[0]
    local_feat = query_vectors.shape[1]
    head_count = local_feat // HD
    inverse = 1.0 / math.sqrt(HD)
    near_queries = split_heads(query_vectors, head_count)
    near_tangents = split_heads(tangent_queries, head_count)
    near_keys = split_heads(key_vectors, head_count)
    near_values = split_heads(value_vectors, head_count)
    row_zeros = jnp.zeros((local_rows, head_count), jnp.float32)
    sum_zeros = jnp.zeros((local_rows, head_count, HD), jnp.float32)
    stats_start = (
        jnp.full((local_rows, head_count), floor_value, jnp.float32),
        row_zeros,
        row_zeros,
        sum_zeros,
        sum_zeros,
    )
    extra_start = ()
    shards = (
        lax.all_gather(key_vectors, "blk", axis=0, tiled=True),
        lax.all_gather(value_vectors, "blk", axis=0, tiled=True),
        lax.all_gather(tangent_keys, "blk", axis=0, tiled=True),
        lax.all_gather(tangent_values, "blk", axis=0, tiled=True),
    )
    stats = stats_start
    extras = extra_start
    operands = tuple((split_heads(member, head_count) for member in shards))
    stats = fold_blocks(
        partial(forward_update, (near_queries, near_tangents, inverse)),
        stats,
        operands,
        shards[0].shape[0],
    )
    stats, extras = (stats, extras)
    row_peak, denominator, tan_weight, primal_sum, tangent_sum = stats
    primal = primal_sum / denominator[:, :, None]
    tangent = (
        tangent_sum / denominator[:, :, None] - (tan_weight / denominator)[:, :, None] * primal
    )
    primal_low = primal.astype(jnp.bfloat16)
    tangent_low = tangent.astype(jnp.bfloat16).reshape(local_rows, -1)
    primal_out, tangent_out = (
        lax.all_to_all(
            primal_low.reshape(local_rows, -1), "head", split_axis=0, concat_axis=1, tiled=True
        ),
        lax.all_to_all(tangent_low, "head", split_axis=0, concat_axis=1, tiled=True),
    )
    token_cotangent = (
        scale_loss * (target_gap.astype(jnp.float32) + tangent_out.astype(jnp.float32))
    ).astype(jnp.bfloat16)
    cotangent = lax.all_to_all(token_cotangent, "head", split_axis=1, concat_axis=0, tiled=True)
    near_cotangent = split_heads(cotangent, head_count)
    log_total = row_peak + jnp.log(denominator)
    inner_sums = jnp.sum(
        near_cotangent.astype(jnp.float32) * primal_low.astype(jnp.float32), axis=2
    )
    all_log, all_inner = (
        lax.all_gather(log_total, "blk", axis=0, tiled=True),
        lax.all_gather(inner_sums, "blk", axis=0, tiled=True),
    )
    query_nearby = (near_queries, near_cotangent, log_total, inner_sums, inverse)
    key_nearby = (near_keys, near_values, inverse)
    shards = (
        lax.all_gather(key_vectors, "blk", axis=0, tiled=True),
        lax.all_gather(value_vectors, "blk", axis=0, tiled=True),
        lax.all_gather(query_vectors, "blk", axis=0, tiled=True),
        lax.all_gather(cotangent, "blk", axis=0, tiled=True),
    )
    query_acc = sum_zeros
    key_acc = sum_zeros
    value_acc = sum_zeros
    length = shards[0].shape[0]
    far_keys, far_values, far_queries, far_cotangent = tuple(
        (split_heads(member, head_count) for member in shards)
    )
    query_acc = fold_blocks(
        partial(query_update, query_nearby), query_acc, (far_keys, far_values), length
    )
    key_acc, value_acc = fold_blocks(
        partial(key_update, key_nearby),
        (key_acc, value_acc),
        (far_queries, far_cotangent, all_log, all_inner),
        length,
    )
    query_acc, key_acc, value_acc = (query_acc, key_acc, value_acc)
    query_grad = (query_acc * inverse).astype(jnp.bfloat16).reshape(local_rows, -1)
    key_grad = (key_acc * inverse).astype(jnp.bfloat16).reshape(local_rows, -1)
    value_grad = value_acc.astype(jnp.bfloat16).reshape(local_rows, -1)
    return (primal_out, tangent_out, query_grad, key_grad, value_grad)


def solution(mesh):
    return jax.shard_map(
        per_device,
        mesh=mesh,
        in_specs=(
            P("blk", "head"),
            P("blk", "head"),
            P("blk", "head"),
            P("blk", "head"),
            P("blk", "head"),
            P("blk", "head"),
            P(("blk", "head"), None),
        ),
        out_specs=(
            P(("blk", "head"), None),
            P(("blk", "head"), None),
            P("blk", "head"),
            P("blk", "head"),
            P("blk", "head"),
        ),
        check_vma=False,
    )
```

profile of v0, /device:TPU:78, one launch (start us, length us, event | category | flops | bytes accessed | tf_op | source)
XLA Modules:
  0.0 1064.1 jit_solution(17173733373195373709)
XLA Ops:
  7.2 1.8 copy.145
  9.9 1.7 copy.149
  11.7 1.7 copy.148
  14.2 140.8 %all-gather.7.cloned.1.call-done = bf16[4096,640]{0,1:T(8,128)(2,1)} async-done(((bf16[128,640]{0,1:T(8,128)(2,1)}), bf16[4096,640]{0,1:T(8,128)(2,1)}) %all-gather.7.cloned.1.call-update) | async-done | bytes 5242896 | tf_op jit(solution)/shard_map/all_gather | solution.py:138
  155.0 7.9 copy.151
  162.8 143.4 %all-gather.13.cloned.1.call-done = bf16[4096,640]{1,0:T(8,128)(2,1)} async-done(((bf16[128,640]{1,0:T(8,128)(2,1)}), bf16[4096,640]{1,0:T(8,128)(2,1)}) %all-gather.13.cloned.1.call-update) | async-done | bytes 5242896 | tf_op jit(solution)/shard_map/all_gather | solution.py:141
  306.3 8.0 copy.150
  314.2 148.9 %all-gather.11.cloned.1.call-done = bf16[4096,640]{0,1:T(8,128)(2,1)} async-done(((bf16[128,640]{0,1:T(8,128)(2,1)}), bf16[4096,640]{0,1:T(8,128)(2,1)}) %all-gather.11.cloned.1.call-update) | async-done | bytes 5242896 | tf_op jit(solution)/shard_map/all_gather | solution.py:139
  463.1 146.8 %all-gather.9.cloned.1.call-done = bf16[4096,640]{0,1:T(8,128)(2,1)} async-done(((bf16[128,640]{0,1:T(8,128)(2,1)}), bf16[4096,640]{0,1:T(8,128)(2,1)}) %all-gather.9.cloned.1.call-update) | async-done | bytes 5242896 | tf_op jit(solution)/shard_map/all_gather | solution.py:140
  609.9 73.8 %while.52 = (s32[]{:T(128)}, f32[128,5]{0,1:T(8,128)S(1)}, f32[128,5]{0,1:T(8,128)S(1)}, f32[128,5]{0,1:T(8,128)S(1)}, f32[128,5,128]{0,2,1:T(8,128)S(1)}, /*ind...) while((s32[]{:T(128)}, f32[128,5]{0,1:T(8,128)S(1)}, ...), condition=%wide.region_4.0_spmd.clone, body=%wide.region_0.0_spmd.clone.sunk | while | flops 508481920 | bytes 16937192 | solution.py:32
  612.8 1.7 fusion.126
  615.9 1.5 fusion.130
  617.4 1.5 fusion.129
  622.0 1.7 fusion.126
  631.2 1.7 fusion.126
  634.4 1.5 fusion.130
  640.5 1.7 fusion.126
  649.7 1.7 fusion.126
  652.9 1.5 fusion.130
  658.9 1.7 fusion.126
  668.1 1.7 fusion.126
  677.4 1.7 fusion.126
  685.0 8.1 all_to_all.57
  693.2 9.5 all_to_all.58
  703.7 63.6 %all_gather.31 = f32[4096,5]{0,1:T(8,128)S(1)} all-gather(f32[128,5]{0,1:T(8,128)S(1)} %get-tuple-element.1071), channel_id=1, replica_groups=mesh['blk'=32,'head'=4] {'blk'}, dimensions={0}, use_global_device_ids=true | all-gather | bytes 84480 | tf_op jit(solution)/shard_map/all_gather | solution.py:176
  768.9 106.4 %all_gather.33 = f32[4096,5]{1,0:T(8,128)} all-gather(f32[128,5]{1,0:T(8,128)S(1)} %get-tuple-element.814), channel_id=1, replica_groups=mesh['blk'=32,'head'=4] {'blk'}, dimensions={0}, use_global_device_ids=true | all-gather | bytes 84480 | tf_op jit(solution)/shard_map/all_gather | solution.py:177
  875.2 2.2 copy.175
  878.4 4.8 all-to-all-start
  883.2 28.4 %while.53 = (s32[]{:T(128)}, f32[128,5,128]{0,2,1:T(8,128)S(1)}, bf16[4096,5,128]{2,0,1:T(8,128)(2,1)}, bf16[128,5,128]{2,0,1:T(8,128)(2,1)S(1)}, f32[128,5]{0,1...) while((s32[]{:T(128)}, f32[128,5,128]{0,2,1:T(8,128)S(1)}, ...), condition=%wide.region_7.0_spmd.clone, body=%wide.region_6.0_spmd.clone.sunk | while | flops 253460480 | bytes 5577392 | solution.py:32
  883.2 1.5 fusion.136
  884.6 2.0 fusion.137
  886.7 1.5 fusion.136
  888.2 2.0 fusion.137
  890.2 1.5 fusion.136
  891.7 2.0 fusion.137
  893.8 1.5 fusion.136
  895.3 2.1 fusion.137
  897.4 1.5 fusion.136
  898.9 2.0 fusion.137
  900.9 1.5 fusion.136
  902.4 2.0 fusion.137
  904.5 1.5 fusion.136
  906.0 2.1 fusion.137
  908.0 1.5 fusion.136
  909.5 2.0 fusion.137
  913.1 8.0 copy.169
  921.1 91.7 %all-gather.15.cloned.1.call-done = bf16[4096,640]{0,1:T(8,128)(2,1)} async-done(((bf16[128,640]{0,1:T(8,128)(2,1)}), bf16[4096,640]{0,1:T(8,128)(2,1)}) %all-gather.15.cloned.1.call-update) | async-done | bytes 5242896 | tf_op jit(solution)/shard_map/all_gather | solution.py:184
  1012.8 42.7 %while.54 = (s32[]{:T(128)}, f32[128,5,128]{0,2,1:T(8,128)S(1)}, f32[128,5,128]{0,2,1:T(8,128)S(1)}, bf16[4096,5,128]{0,2,1:T(8,128)(2,1)}, bf16[128,5,128]{2,0,...) while((s32[]{:T(128)}, f32[128,5,128]{0,2,1:T(8,128)S(1)}, ...), condition=%wide.region_9.0_spmd.clone, body=%wide.region_8.0_spmd.clone.sunk | while | flops 337838080 | bytes 8255169 | solution.py:32
  1012.8 1.7 fusion.145
  1016.0 2.1 fusion.146
  1018.2 1.7 fusion.145
  1021.3 2.1 fusion.146
  1023.5 1.7 fusion.145
  1026.7 2.1 fusion.146
  1028.9 1.7 fusion.145
  1032.0 2.1 fusion.146
  1034.2 1.7 fusion.145
  1037.4 2.1 fusion.146
  1039.6 1.7 fusion.145
  1042.7 2.1 fusion.146
  1044.9 1.7 fusion.145
  1048.1 2.1 fusion.146
  1050.2 1.7 fusion.145
  1053.4 2.1 fusion.146
  (156 shorter events, 75.0 us)
Async XLA Ops:
  7.2 6.3 copy-start.4
  7.2 6.7 copy-start.5
  7.2 147.8 %all-gather.7.cloned.1.call-start = ((), (), s32[]{:S(2)}) async-start(), calls=%async_computation.3 | async-start | bytes 5406720 | tf_op jit(solution)/shard_map/all_gather | solution.py:138
  9.1 297.2 %all-gather.13.cloned.1.call-start = ((), (), s32[]{:S(2)}) async-start(), calls=%async_computation.6 | async-start | bytes 5406720 | tf_op jit(solution)/shard_map/all_gather | solution.py:141
  9.8 453.3 %all-gather.11.cloned.1.call-start = ((), (), s32[]{:S(2)}) async-start(), calls=%async_computation.5 | async-start | bytes 5406720 | tf_op jit(solution)/shard_map/all_gather | solution.py:139
  11.6 598.3 %all-gather.9.cloned.1.call-start = ((), (), s32[]{:S(2)}) async-start(), calls=%async_computation.4 | async-start | bytes 5406720 | tf_op jit(solution)/shard_map/all_gather | solution.py:140
  13.4 899.7 %all-gather.17.cloned.1.call-start = ((), (), s32[]{:S(2)}) async-start(), calls=%async_computation.8 | async-start | bytes 5406720 | tf_op jit(solution)/shard_map/all_gather | solution.py:185
  13.7 149.2 %copy-start = (bf16[128,640]{0,1:T(8,128)(2,1)}, bf16[128,640]{0,1:T(8,128)(2,1)S(1)}, u32[]{:S(2)}) copy-start(bf16[128,640]{0,1:T(8,128)(2,1)S(1)} %copy.146) | copy-start | bytes 491524
  684.4 8.7 copy-start.6
  684.8 18.6 %copy-start.1 = (bf16[128,640]{0,1:T(8,128)(2,1)S(1)}, bf16[128,640]{0,1:T(8,128)(2,1)}, u32[]{:S(2)}) copy-start(bf16[128,640]{0,1:T(8,128)(2,1)} %copy.145) | copy-start | bytes 491524
  685.0 18.5 %copy-start.2 = (bf16[128,640]{0,1:T(8,128)(2,1)S(1)}, bf16[128,640]{0,1:T(8,128)(2,1)}, u32[]{:S(2)}) copy-start(bf16[128,640]{0,1:T(8,128)(2,1)} %copy.149) | copy-start | bytes 491524
  693.1 75.3 %copy-start.3 = (bf16[4,4,8,640]{3,2,0,1:T(8,128)(2,1)}, bf16[4,4,8,640]{3,2,0,1:T(8,128)(2,1)S(1)}, u32[]{:S(2)}) copy-start(bf16[4,4,8,640]{3,2,0,1:T(8,128)(2,1)S(1)} %copy.192) | copy-start | bytes 491524
  702.7 310.1 %all-gather.15.cloned.1.call-start = ((), (), s32[]{:S(2)}) async-start(), calls=%async_computation.7 | async-start | bytes 5406720 | tf_op jit(solution)/shard_map/all_gather | solution.py:184
  878.4 34.1 %all-to-all-start = ((bf16[4,32,640]{2,1,0:T(8,128)(2,1)}), bf16[4,32,640]{2,1,0:T(8,128)(2,1)S(1)}, u32[]{:S(2)}, u32[]{:S(2)}) async-start(bf16[4,32,640]{2,1,0:T(8,128)(2,1)} %all_to_all.42), calls=%async_computation | async-start | bytes 327680 | tf_op jit(solution)/shard_map/all_to_all | solution.py:161
Sparse Core Ops, SparseCore 0:
  10.1 144.7 all-gather.6
  156.6 149.6 all-gather.12
  308.4 154.6 all-gather.10
  465.1 144.7 all-gather.8
  702.8 152.3 all-gather.16
  856.6 156.1 all-gather.14
where the time goes:
time: 1070 us; the launch traced here: 1060 us
  waiting for transfers between devices  673 us (63%)
  blocking collectives  188 us (18%)
  matrix products  142 us (13%)
  local copies, waits for them, and re-layouts  38.6 us (4%)
  between operations  14.4 us (1%)
    all_gather x1, waiting for transfers between devices, per_device(): lax.all_gather(value_vectors, 'blk', axis=0, tiled=True)  149 us
    all_gather x1, waiting for transfers between devices, per_device(): lax.all_gather(tangent_keys, 'blk', axis=0, tiled=True)  147 us
    all_gather x1, waiting for transfers between devices, per_device(): lax.all_gather(tangent_values, 'blk', axis=0, tiled=True)  143 us
    all_gather x1, waiting for transfers between devices, per_device(): lax.all_gather(key_vectors, 'blk', axis=0, tiled=True)  141 us
    all_gather x1, blocking collectives, per_device(): lax.all_gather(inner_sums, 'blk', axis=0, tiled=True)  106 us
    all_gather x1, waiting for transfers between devices, per_device(): lax.all_gather(query_vectors, 'blk', axis=0, tiled=True)  91.7 us
    all_gather x1, blocking collectives, per_device(): lax.all_gather(log_total, 'blk', axis=0, tiled=True)  63.6 us
  transfers between devices with their start and end apart: 7, of which 5 were waited for; matrix products, arithmetic and copies ran while one was open for 6% of the time, Pallas kernels for 0%

commit v1 on v0

--- a/solution.py
+++ b/solution.py
@@ -134,9 +134,19 @@
         sum_zeros,
     )
     extra_start = ()
+
+    def test_node(frame):
+        base_arr = jnp.concatenate(
+            lax.all_to_all(
+                jnp.stack([frame] * lax.axis_size("blk")), "blk", split_axis=0, concat_axis=0
+            ),
+            axis=0,
+        )
+        return base_arr
+
     shards = (
         lax.all_gather(key_vectors, "blk", axis=0, tiled=True),
-        lax.all_gather(value_vectors, "blk", axis=0, tiled=True),
+        test_node(value_vectors),
         lax.all_gather(tangent_keys, "blk", axis=0, tiled=True),
         lax.all_gather(tangent_values, "blk", axis=0, tiled=True),
     )

time: 1070 us -> 1020 us (0.953)
  waiting for transfers between devices: 673 us -> 588 us
  local copies, waits for them, and re-layouts: 38.6 us -> 58.4 us
    all_gather x1, waiting for transfers between devices: 149 us -> 0.01 us  [per_device(): lax.all_gather(value_vectors, 'blk', axis=0, tiled=True)]
    all_to_all x0 -> x1, waiting for transfers between devices: none -> 78.4 us  [test_node(): lax.all_to_all(jnp.stack([frame] * lax.axis_size('blk')), 'blk', split_ax...]
    all_gather x1, waiting for transfers between devices: 141 us -> 77.8 us  [per_device(): lax.all_gather(key_vectors, 'blk', axis=0, tiled=True)]
    all_gather x1, waiting for transfers between devices: 91.7 us -> 137 us  [per_device(): lax.all_gather(query_vectors, 'blk', axis=0, tiled=True)]
    another operation x0 -> x2, local copies, waits for them, and re-layouts: none -> 12.4 us  [the longest x1 8.86 us: split_heads(): matrix.reshape(matrix.shape[0], head_count, matrix.shape[1] // head_count)]
  transfers between devices with their start and end apart: 7 -> 8, of which waited for: 5 -> 5; matrix products, arithmetic and copies ran while one was open for 6% -> 15% of each run, Pallas kernels for 0% -> 0%
where the time goes in v1:
time: 1020 us
  waiting for transfers between devices  588 us (58%)
  blocking collectives  195 us (19%)
  matrix products  142 us (14%)
  local copies, waits for them, and re-layouts  58.4 us (6%)
  between operations  14.4 us (1%)
  starting transfers between devices  13.7 us (1%)
    all_gather x1, waiting for transfers between devices, per_device(): lax.all_gather(tangent_keys, 'blk', axis=0, tiled=True)  149 us
    all_gather x1, waiting for transfers between devices, per_device(): lax.all_gather(tangent_values, 'blk', axis=0, tiled=True)  144 us
    all_gather x1, waiting for transfers between devices, per_device(): lax.all_gather(query_vectors, 'blk', axis=0, tiled=True)  137 us
    all_gather x1, blocking collectives, per_device(): lax.all_gather(inner_sums, 'blk', axis=0, tiled=True)  113 us
    all_to_all x1, waiting for transfers between devices, test_node(): lax.all_to_all(jnp.stack([frame] * lax.axis_size('blk')), 'blk', split_ax...  78.4 us
    all_gather x1, waiting for transfers between devices, per_device(): lax.all_gather(key_vectors, 'blk', axis=0, tiled=True)  77.8 us
    all_gather x1, blocking collectives, per_device(): lax.all_gather(log_total, 'blk', axis=0, tiled=True)  64.6 us
  transfers between devices with their start and end apart: 8, of which 5 were waited for; matrix products, arithmetic and copies ran while one was open for 15% of the time, Pallas kernels for 0%

profile of v1, /device:TPU:78, one launch (start us, length us, event | category | flops | bytes accessed | tf_op | source)
XLA Modules:
  0.0 1016.1 jit_solution(18047807967926515273)
XLA Ops:
  7.2 1.7 copy.190
  9.8 1.7 copy.193
  12.6 3.6 stack.2
  16.2 8.7 all-to-all-start
  26.2 78.4 %all-to-all-done = bf16[32,128,640]{1,2,0:T(8,128)(2,1)} async-done(((bf16[32,128,640]{1,2,0:T(8,128)(2,1)}), bf16[32,128,640]{1,2,0:T(8,128)(2,1)}, u32[]{:S(2)}, u32[]{:S(2)}) %all-to-all-start) | async-done | bytes 5242912 | tf_op jit(solution)/shard_map/all_to_all | solution.py:140
  104.6 8.2 copy.195
  112.8 8.9 reshape_reshape.3
  121.7 77.8 %all-gather.7.cloned.1.call-done = bf16[4096,640]{0,1:T(8,128)(2,1)} async-done(((bf16[128,640]{0,1:T(8,128)(2,1)}), bf16[4096,640]{0,1:T(8,128)(2,1)}) %all-gather.7.cloned.1.call-update) | async-done | bytes 5242896 | tf_op jit(solution)/shard_map/all_gather | solution.py:148
  199.4 7.8 copy.197
  207.3 144.4 %all-gather.11.cloned.1.call-done = bf16[4096,640]{1,0:T(8,128)(2,1)} async-done(((bf16[128,640]{1,0:T(8,128)(2,1)}), bf16[4096,640]{1,0:T(8,128)(2,1)}) %all-gather.11.cloned.1.call-update) | async-done | bytes 5242896 | tf_op jit(solution)/shard_map/all_gather | solution.py:151
  351.7 7.9 copy.196
  359.6 148.9 %all-gather.9.cloned.1.call-done = bf16[4096,640]{0,1:T(8,128)(2,1)} async-done(((bf16[128,640]{0,1:T(8,128)(2,1)}), bf16[4096,640]{0,1:T(8,128)(2,1)}) %all-gather.9.cloned.1.call-update) | async-done | bytes 5242896 | tf_op jit(solution)/shard_map/all_gather | solution.py:150
  508.5 74.0 %while.52 = (s32[]{:T(128)}, f32[128,5]{0,1:T(8,128)S(1)}, f32[128,5]{0,1:T(8,128)S(1)}, f32[128,5]{0,1:T(8,128)S(1)}, f32[128,5,128]{0,2,1:T(8,128)S(1)}, /*ind...) while((s32[]{:T(128)}, f32[128,5]{0,1:T(8,128)S(1)}, ...), condition=%wide.region_4.0_spmd.clone, body=%wide.region_0.0_spmd.clone.sunk | while | flops 508481920 | bytes 16937192 | solution.py:32
  511.4 1.7 fusion.126
  520.6 1.7 fusion.126
  529.9 1.7 fusion.126
  539.1 1.7 fusion.126
  548.4 1.7 fusion.126
  557.6 1.7 fusion.126
  559.3 1.5 convolution_bitcast_fusion.7
  566.9 1.7 fusion.126
  576.1 1.7 fusion.126
  583.8 8.1 all_to_all.62
  592.0 9.5 all_to_all.63
  602.5 64.6 %all_gather.30 = f32[4096,5]{0,1:T(8,128)S(1)} all-gather(f32[128,5]{0,1:T(8,128)S(1)} %get-tuple-element.1105), channel_id=1, replica_groups=mesh['blk'=32,'head'=4] {'blk'}, dimensions={0}, use_global_device_ids=true | all-gather | bytes 84480 | tf_op jit(solution)/shard_map/all_gather | solution.py:186
  668.7 112.7 %all_gather.32 = f32[4096,5]{1,0:T(8,128)} all-gather(f32[128,5]{1,0:T(8,128)S(1)} %get-tuple-element.848), channel_id=1, replica_groups=mesh['blk'=32,'head'=4] {'blk'}, dimensions={0}, use_global_device_ids=true | all-gather | bytes 84480 | tf_op jit(solution)/shard_map/all_gather | solution.py:187
  781.4 2.2 copy.222
  784.5 4.8 all-to-all-start.1
  789.3 28.6 %while.53 = (s32[]{:T(128)}, f32[128,5,128]{0,2,1:T(8,128)S(1)}, bf16[4096,5,128]{2,0,1:T(8,128)(2,1)}, bf16[128,5,128]{2,0,1:T(8,128)(2,1)S(1)}, f32[128,5]{0,1...) while((s32[]{:T(128)}, f32[128,5,128]{0,2,1:T(8,128)S(1)}, ...), condition=%wide.region_7.0_spmd.clone, body=%wide.region_6.0_spmd.clone.sunk | while | flops 253460480 | bytes 5577392 | solution.py:32
  789.3 1.5 fusion.136
  790.8 2.1 fusion.137
  792.9 1.5 fusion.136
  794.4 2.1 fusion.137
  796.6 1.5 fusion.136
  798.1 2.0 fusion.137
  800.1 1.5 fusion.136
  801.6 2.1 fusion.137
  803.8 1.5 fusion.136
  805.3 2.0 fusion.137
  807.3 1.5 fusion.136
  808.8 2.0 fusion.137
  810.9 1.5 fusion.136
  812.3 2.0 fusion.137
  814.4 1.5 fusion.136
  815.9 2.0 fusion.137
  819.5 8.0 copy.216
  827.5 137.3 %all-gather.15.cloned.1.call-done = bf16[4096,640]{0,1:T(8,128)(2,1)} async-done(((bf16[128,640]{0,1:T(8,128)(2,1)}), bf16[4096,640]{0,1:T(8,128)(2,1)}) %all-gather.15.cloned.1.call-update) | async-done | bytes 5242896 | tf_op jit(solution)/shard_map/all_gather | solution.py:194
  964.7 42.8 %while.54 = (s32[]{:T(128)}, f32[128,5,128]{0,2,1:T(8,128)S(1)}, f32[128,5,128]{0,2,1:T(8,128)S(1)}, bf16[4096,5,128]{0,2,1:T(8,128)(2,1)}, bf16[128,5,128]{2,0,...) while((s32[]{:T(128)}, f32[128,5,128]{0,2,1:T(8,128)S(1)}, ...), condition=%wide.region_9.0_spmd.clone, body=%wide.region_8.0_spmd.clone.sunk | while | flops 337838080 | bytes 8255169 | solution.py:32
  964.8 1.7 fusion.145
  967.9 2.1 fusion.146
  970.1 1.7 fusion.145
  973.3 2.1 fusion.146
  975.4 1.7 fusion.145
  978.6 2.1 fusion.146
  980.8 1.7 fusion.145
  984.0 2.1 fusion.146
  986.1 1.7 fusion.145
  989.3 2.1 fusion.146
  991.5 1.7 fusion.145
  994.7 2.1 fusion.146
  996.8 1.7 fusion.145
  1000.0 2.1 fusion.146
  1002.2 1.7 fusion.145
  1005.4 2.1 fusion.146
  (163 shorter events, 81.1 us)
Async XLA Ops:
  7.2 192.3 %all-gather.7.cloned.1.call-start = ((), (), s32[]{:S(2)}) async-start(), calls=%async_computation.4 | async-start | bytes 5406720 | tf_op jit(solution)/shard_map/all_gather | solution.py:148
  9.0 342.7 %all-gather.11.cloned.1.call-start = ((), (), s32[]{:S(2)}) async-start(), calls=%async_computation.6 | async-start | bytes 5406720 | tf_op jit(solution)/shard_map/all_gather | solution.py:151
  9.7 498.8 %all-gather.9.cloned.1.call-start = ((), (), s32[]{:S(2)}) async-start(), calls=%async_computation.5 | async-start | bytes 5406720 | tf_op jit(solution)/shard_map/all_gather | solution.py:150
  12.6 3.6 copy-start
  16.2 9.4 copy-start.5
  16.2 9.7 copy-start.6
  16.2 88.5 %all-to-all-start = ((bf16[32,128,640]{1,2,0:T(8,128)(2,1)}), bf16[32,128,640]{1,2,0:T(8,128)(2,1)}, u32[]{:S(2)}, u32[]{:S(2)}) async-start(bf16[32,128,640]{1,2,0:T(8,128)(2,1)} %stack.2), calls=%async_computation | async-start | bytes 10485760 | tf_op jit(solution)/shard_map/all_to_all | solution.py:140
  24.9 764.5 %all-gather.13.cloned.1.call-start = ((), (), s32[]{:S(2)}) async-start(), calls=%async_computation.7 | async-start | bytes 5406720 | tf_op jit(solution)/shard_map/all_gather | solution.py:193
  25.4 794.0 %all-gather.17.cloned.1.call-start = ((), (), s32[]{:S(2)}) async-start(), calls=%async_computation.9 | async-start | bytes 5406720 | tf_op jit(solution)/shard_map/all_gather | solution.py:195
  25.7 87.1 %copy-start.2 = (bf16[128,640]{0,1:T(8,128)(2,1)}, bf16[128,640]{0,1:T(8,128)(2,1)S(1)}, u32[]{:S(2)}) copy-start(bf16[128,640]{0,1:T(8,128)(2,1)S(1)} %copy.191) | copy-start | bytes 491524
  583.2 8.7 copy-start.7
  583.6 18.6 %copy-start.1 = (bf16[128,640]{0,1:T(8,128)(2,1)S(1)}, bf16[128,640]{0,1:T(8,128)(2,1)}, u32[]{:S(2)}) copy-start(bf16[128,640]{0,1:T(8,128)(2,1)} %copy-done) | copy-start | bytes 491524
  583.8 18.5 %copy-start.3 = (bf16[128,640]{0,1:T(8,128)(2,1)S(1)}, bf16[128,640]{0,1:T(8,128)(2,1)}, u32[]{:S(2)}) copy-start(bf16[128,640]{0,1:T(8,128)(2,1)} %copy.190) | copy-start | bytes 491524
  591.9 76.4 %copy-start.4 = (bf16[4,4,8,640]{3,2,0,1:T(8,128)(2,1)}, bf16[4,4,8,640]{3,2,0,1:T(8,128)(2,1)S(1)}, u32[]{:S(2)}) copy-start(bf16[4,4,8,640]{3,2,0,1:T(8,128)(2,1)S(1)} %copy.239) | copy-start | bytes 491524
  601.5 363.2 %all-gather.15.cloned.1.call-start = ((), (), s32[]{:S(2)}) async-start(), calls=%async_computation.8 | async-start | bytes 5406720 | tf_op jit(solution)/shard_map/all_gather | solution.py:194
  784.5 34.3 %all-to-all-start.1 = ((bf16[4,32,640]{2,1,0:T(8,128)(2,1)}), bf16[4,32,640]{2,1,0:T(8,128)(2,1)S(1)}, u32[]{:S(2)}, u32[]{:S(2)}) async-start(bf16[4,32,640]{2,1,0:T(8,128)(2,1)} %all_to_all.46), calls=%async_computation.1 | async-start | bytes 327680 | tf_op jit(solution)/shard_map/all_to_all | solution.py:171
Sparse Core Ops, SparseCore 0:
  10.1 189.2 all-gather.6
  201.1 150.5 all-gather.10
  353.8 154.6 all-gather.8
  510.5 145.3 all-gather.12
  657.4 151.8 all-gather.16
  810.8 153.9 all-gather.14
